TPU v7x, 32 devices: a whole 2x2x4 slice. The times are simulated.
32 devices in a mesh: section: 4 (over z), th: 4 (over y, x), tw: 2 (over core).
Axes of the slice: x: 2, y: 2, z: 4, core: 2. Of those that a mesh axis runs over, the one named last changes fastest.
Arguments:
- features: bfloat16 [16, 64, 64, 128], P('section', 'th', 'tw'), may hold values from -11 to 11, as said below
- norm_gain: float32 [128], replicated, may hold values from 0.25 to 1.75
- norm_shift: float32 [128], replicated, may hold values from -3 to 3
- first_kernel: bfloat16 [3, 3, 3, 128, 128], replicated, may hold values from -0.109375 to 0.109375
- second_gain: float32 [128], replicated, may hold values from 0.25 to 1.75
- second_shift: float32 [128], replicated, may hold values from -3 to 3
- second_kernel: bfloat16 [3, 3, 3, 128, 128], replicated, may hold values from -0.109375 to 0.109375
Outputs:
- block_out: bfloat16 [16, 64, 64, 128], P('section', 'th', 'tw')
Inputs may be any that keep to these rules, and one draw needn't show every extreme that they name: `features`: activations of order one.
All inputs are finite; a program needn't handle non-finite values.
Results may differ from a plain program's by a relative error of at most 0.0038.
Values may be sent and summed in bfloat16 or wider, within the bound.
A program may use at most 128 MiB of HBM per device.

v0:
```python
import jax
import jax.numpy as jnp
from jax import lax
from jax.sharding import PartitionSpec as P

GROUPS = 32


def passed_along(value, axis, steps):
    count = lax.axis_size(axis)
    initial, last = (max(0, -steps), min(count, count - steps))
    return lax.ppermute(value, axis, [(source, source + steps) for source in range(initial, last)])


def extended(cells, sides, width):
    for axis, dim in sides:
        count = lax.axis_size(axis)
        ends = count - 1
        head = lax.slice_in_dim(cells, 0, width, axis=dim)
        tail = lax.slice_in_dim(cells, cells.shape[dim] - width, cells.shape[dim], axis=dim)
        cells = jnp.concatenate(
            [
                lax.ppermute(tail, axis, [(i, (i + 1) % count) for i in range(ends)]),
                cells,
                lax.ppermute(head, axis, [((i + 1) % count, i) for i in range(ends)]),
            ],
            axis=dim,
        )
    return cells


def causal_conv(padded, kernel):
    frames = padded.shape[0] - 2
    rows = padded.shape[1] - 2
    cols = padded.shape[2] - 2
    chans = padded.shape[3]
    stacked = jnp.concatenate([padded[:, :, d : d + cols, :] for d in range(3)], axis=-1)
    taps = kernel.reshape(3, 3, 3 * chans, kernel.shape[-1])
    total = jnp.zeros((frames * rows * cols, kernel.shape[-1]), jnp.float32)
    for dt in range(3):
        for dh in range(3):
            window = stacked[dt : dt + frames, dh : dh + rows].reshape(-1, 3 * chans)
            total = total + jnp.dot(window, taps[dt, dh], preferred_element_type=jnp.float32)
    return total.reshape(frames, rows, cols, kernel.shape[-1])


def group_totals(values):
    chans = values.shape[-1]
    return jnp.sum(values.reshape(-1, GROUPS, chans // GROUPS), axis=(0, 2))


def group_moments(interior):
    chans = interior.shape[-1]
    count = (
        interior.size
        // GROUPS
        * lax.axis_size("section")
        * lax.axis_size("th")
        * lax.axis_size("tw")
    )
    first, second = lax.psum(
        (group_totals(interior), group_totals(interior * interior)), ("section", "th", "tw")
    )
    mean = first / count
    var = second / count - mean * mean
    return (jnp.repeat(mean, chans // GROUPS), jnp.repeat(var, chans // GROUPS))


def normalize_act(values, moments, gain, shift):
    mean, var = moments
    normed = (values - mean) / jnp.sqrt(var + 1e-06) * gain + shift
    return jax.nn.silu(normed).astype(jnp.bfloat16)


def extend_each(act):
    earlier = passed_along(act[-2:], "section", 1)
    longer = jnp.concatenate([earlier, act], axis=0)
    return extended(longer, (("th", 1), ("tw", 2)), 1)


def shards(features, norm_gain, norm_shift, first_kernel, second_gain, second_shift, second_kernel):
    inputs = features.astype(jnp.float32)
    first_act = normalize_act(inputs, group_moments(inputs), norm_gain, norm_shift)
    hidden = causal_conv(extend_each(first_act), first_kernel)
    second_act = normalize_act(hidden, group_moments(hidden), second_gain, second_shift)
    second_padded = extend_each(second_act)
    branch = causal_conv(second_padded, second_kernel)
    return (inputs + branch).astype(jnp.bfloat16)


def solution(mesh):
    placed = (P("section", "th", "tw", None), P(), P(), P(), P(), P(), P())
    return jax.shard_map(
        shards,
        mesh=mesh,
        in_specs=placed,
        out_specs=P("section", "th", "tw", None),
        check_vma=False,
    )
```

profile of v0, /device:TPU:0, one launch (start us, length us, event | category | flops | bytes accessed | tf_op | source)
XLA Modules:
  0.0 157.2 jit_solution(16403487780932922841)
XLA Ops:
  0.0 1.3 convert_reduce_fusion
  1.8 42.0 %all-reduce.1 = (f32[32]{0:T(128)S(1)}, f32[32]{0:T(128)S(1)}) all-reduce(f32[32]{0:T(128)S(1)} %reduce_sum.54, f32[32]{0:T(128)S(1)} %reduce_sum.51), channel_id=1, replica_groups=mesh['section'=4,'th'=4,'tw'=2] {'section','th','tw'}, use_global_device_ids=true, to_apply=%region_5.6 | all-reduce | flops 64 | bytes 512 | tf_op jit(solution)/shard_map/psum | solution.py:61
  44.1 1.4 multiply_convert_fusion.1
  45.6 3.4 %collective-permute-start = (bf16[2,16,32,128]{3,2,1,0:T(8,128)(2,1)S(1)}, bf16[2,16,32,128]{3,2,1,0:T(8,128)(2,1)S(1)}, u32[]{:S(2)}, u32[]{:S(2)}) collective-permute-start(bf16[2,16,32,128]{3,2,1,0:T(8,128)(2,1)S(1)} %slice.204), channel_id=1, source_target_pairs={{0,8},{8,16},{16,24},{1,9},{9,17},{17,25},{2,10},{10,18},{18,26},{... | collective-permute-start | bytes 786440 | tf_op jit(solution)/shard_map/ppermute | solution.py:12
  49.0 4.7 %collective-permute-done = bf16[2,16,32,128]{3,2,1,0:T(8,128)(2,1)S(1)} collective-permute-done((bf16[2,16,32,128]{3,2,1,0:T(8,128)(2,1)S(1)}, bf16[2,16,32,128]{3,2,1,0:T(8,128)(2,1)S(1)}, u32[]{:S(2)}, u32[]{:S(2)}) %collective-permute-start) | collective-permute-done | bytes 262176 | tf_op jit(solution)/shard_map/ppermute | solution.py:12
  53.8 3.3 %collective-permute-start.1 = (bf16[6,1,32,128]{3,2,1,0:T(8,128)(2,1)S(1)}, bf16[6,1,32,128]{3,2,1,0:T(8,128)(2,1)S(1)}, u32[]{:S(2)}, u32[]{:S(2)}) collective-permute-start(bf16[6,1,32,128]{3,2,1,0:T(8,128)(2,1)S(1)} %get-tuple-element.37), channel_id=1, source_target_pairs={{0,2},{2,4},{4,6},{1,3},{3,5},{5,7},{8,10},{10,12},{12,14},{9,11},... | collective-permute-start | bytes 147464 | tf_op jit(solution)/shard_map/ppermute | solution.py:23
  57.1 1.3 collective-permute-start.2
  58.8 4.3 %collective-permute-done.2 = bf16[6,1,32,128]{3,2,1,0:T(8,128)(2,1)S(1)} collective-permute-done((bf16[6,1,32,128]{3,2,1,0:T(8,128)(2,1)S(1)}, bf16[6,1,32,128]{3,2,1,0:T(8,128)(2,1)S(1)}, u32[]{:S(2)}, u32[]{:S(2)}) %collective-permute-start.2) | collective-permute-done | bytes 49184 | tf_op jit(solution)/shard_map/ppermute | solution.py:25
  63.2 1.3 collective-permute-start.3
  64.5 1.3 collective-permute-start.4
  65.8 1.8 %collective-permute-done.4 = bf16[6,18,1,128]{3,2,1,0:T(2,128)(2,1)S(1)} collective-permute-done((bf16[6,18,1,128]{3,2,1,0:T(2,128)(2,1)S(1)}, bf16[6,18,1,128]{3,2,1,0:T(2,128)(2,1)S(1)}, u32[]{:S(2)}, u32[]{:S(2)}) %collective-permute-start.4) | collective-permute-done | bytes 27680 | tf_op jit(solution)/shard_map/ppermute | solution.py:25
  67.6 4.5 %fusion.2 = bf16[6,18,32,384]{3,2,1,0:T(8,128)(2,1)S(1)} fusion(bf16[6,18,1,128]{3,2,1,0:T(2,128)(2,1)S(1)} %collective-permute-done.4, bf16[6,1,32,128]{3,2,1,0:T(8,128)(2,1)S(1)} %collective-permute-done.2, bf16[6,1,32,128]{3,2,1,0:T(8,128)(2,1)S(1)} %collective-permute-done.1, bf16[4,16,32,128]{3,2,1,0:T(8,128)(2,1)S(1)} %multiply_convert_fusion.1, ...), kind=kLoop, calls=%fused_computation.11 | loop fusion | flops 37158912 | bytes 3594240 | tf_op jit(solution)/shard_map/concatenate | solution.py:37
  72.1 2.2 %fusion.41 = (bf16[4,16,32,384]{3,2,1,0:T(8,128)(2,1)S(1)}, bf16[4,16,32,384]{3,2,1,0:T(8,128)(2,1)S(1)}, bf16[4,16,32,384]{3,2,1,0:T(8,128)(2,1)S(1)}, bf16[4,1...) fusion(bf16[6,18,32,384]{3,2,1,0:T(8,128)(2,1)S(1)} %fusion.2), kind=kLoop, calls=%fused_computation.100 | loop fusion | bytes 28311552 | tf_op jit(solution)/shard_map/slice | solution.py:42
  80.2 40.7 %all-reduce = (f32[32]{0:T(128)S(1)}, f32[32]{0:T(128)S(1)}) all-reduce(f32[32]{0:T(128)S(1)} %reduce_sum.75, f32[32]{0:T(128)S(1)} %reduce_sum.72), channel_id=1, replica_groups=mesh['section'=4,'th'=4,'tw'=2] {'section','th','tw'}, use_global_device_ids=true, to_apply=%region_11.12 | all-reduce | flops 64 | bytes 512 | tf_op jit(solution)/shard_map/psum | solution.py:61
  121.7 2.3 %collective-permute-start.5 = (bf16[2,16,32,128]{3,2,1,0:T(8,128)(2,1)S(1)}, bf16[2,16,32,128]{3,2,1,0:T(8,128)(2,1)S(1)}, u32[]{:S(2)}, u32[]{:S(2)}) collective-permute-start(bf16[2,16,32,128]{3,2,1,0:T(8,128)(2,1)S(1)} %slice.223), channel_id=1, source_target_pairs={{0,8},{8,16},{16,24},{1,9},{9,17},{17,25},{2,10},{10,18},{18,26},{... | collective-permute-start | bytes 786440 | tf_op jit(solution)/shard_map/ppermute | solution.py:12
  124.1 4.7 %collective-permute-done.5 = bf16[2,16,32,128]{3,2,1,0:T(8,128)(2,1)S(1)} collective-permute-done((bf16[2,16,32,128]{3,2,1,0:T(8,128)(2,1)S(1)}, bf16[2,16,32,128]{3,2,1,0:T(8,128)(2,1)S(1)}, u32[]{:S(2)}, u32[]{:S(2)}) %collective-permute-start.5) | collective-permute-done | bytes 262176 | tf_op jit(solution)/shard_map/ppermute | solution.py:12
  128.8 4.6 %collective-permute-start.6 = (bf16[6,1,32,128]{3,2,1,0:T(8,128)(2,1)S(1)}, bf16[6,1,32,128]{3,2,1,0:T(8,128)(2,1)S(1)}, u32[]{:S(2)}, u32[]{:S(2)}) collective-permute-start(bf16[6,1,32,128]{3,2,1,0:T(8,128)(2,1)S(1)} %get-tuple-element.35), channel_id=1, source_target_pairs={{0,2},{2,4},{4,6},{1,3},{3,5},{5,7},{8,10},{10,12},{12,14},{9,11},... | collective-permute-start | bytes 147464 | tf_op jit(solution)/shard_map/ppermute | solution.py:23
  133.4 1.3 collective-permute-start.7
  135.1 4.3 %collective-permute-done.7 = bf16[6,1,32,128]{3,2,1,0:T(8,128)(2,1)S(1)} collective-permute-done((bf16[6,1,32,128]{3,2,1,0:T(8,128)(2,1)S(1)}, bf16[6,1,32,128]{3,2,1,0:T(8,128)(2,1)S(1)}, u32[]{:S(2)}, u32[]{:S(2)}) %collective-permute-start.7) | collective-permute-done | bytes 49184 | tf_op jit(solution)/shard_map/ppermute | solution.py:25
  139.5 1.3 collective-permute-start.8
  140.8 1.5 collective-permute-start.9
  142.3 1.6 %collective-permute-done.9 = bf16[6,18,1,128]{3,2,1,0:T(2,128)(2,1)S(1)} collective-permute-done((bf16[6,18,1,128]{3,2,1,0:T(2,128)(2,1)S(1)}, bf16[6,18,1,128]{3,2,1,0:T(2,128)(2,1)S(1)}, u32[]{:S(2)}, u32[]{:S(2)}) %collective-permute-start.9) | collective-permute-done | bytes 27680 | tf_op jit(solution)/shard_map/ppermute | solution.py:25
  143.9 4.5 %fusion = bf16[6,18,32,384]{3,2,1,0:T(8,128)(2,1)S(1)} fusion(bf16[6,18,1,128]{3,2,1,0:T(2,128)(2,1)S(1)} %collective-permute-done.9, bf16[6,1,32,128]{3,2,1,0:T(8,128)(2,1)S(1)} %collective-permute-done.7, bf16[6,1,32,128]{3,2,1,0:T(8,128)(2,1)S(1)} %collective-permute-done.6, bf16[4,16,32,128]{3,2,1,0:T(8,128)(2,1)S(1)} %multiply_convert_fusion, ...), kind=kLoop, calls=%fused_computation.1 | loop fusion | flops 37158912 | bytes 3594240 | tf_op jit(solution)/shard_map/concatenate | solution.py:37
  148.4 2.2 %fusion.40 = (bf16[4,16,32,384]{3,2,1,0:T(8,128)(2,1)S(1)}, bf16[4,16,32,384]{3,2,1,0:T(8,128)(2,1)S(1)}, bf16[4,16,32,384]{3,2,1,0:T(8,128)(2,1)S(1)}, bf16[4,1...) fusion(bf16[6,18,32,384]{3,2,1,0:T(8,128)(2,1)S(1)} %fusion), kind=kLoop, calls=%fused_computation.99 | loop fusion | bytes 28311552 | tf_op jit(solution)/shard_map/slice | solution.py:42
  (58 shorter events, 15.0 us)
Async XLA Ops:
  45.6 8.2 %collective-permute-start = (bf16[2,16,32,128]{3,2,1,0:T(8,128)(2,1)S(1)}, bf16[2,16,32,128]{3,2,1,0:T(8,128)(2,1)S(1)}, u32[]{:S(2)}, u32[]{:S(2)}) collective-permute-start(bf16[2,16,32,128]{3,2,1,0:T(8,128)(2,1)S(1)} %slice.204), channel_id=1, source_target_pairs={{0,8},{8,16},{16,24},{1,9},{9,17},{17,25},{2,10},{10,18},{18,26},{... | collective-permute-start | bytes 786440 | tf_op jit(solution)/shard_map/ppermute | solution.py:12
  53.8 5.1 %collective-permute-start.1 = (bf16[6,1,32,128]{3,2,1,0:T(8,128)(2,1)S(1)}, bf16[6,1,32,128]{3,2,1,0:T(8,128)(2,1)S(1)}, u32[]{:S(2)}, u32[]{:S(2)}) collective-permute-start(bf16[6,1,32,128]{3,2,1,0:T(8,128)(2,1)S(1)} %get-tuple-element.37), channel_id=1, source_target_pairs={{0,2},{2,4},{4,6},{1,3},{3,5},{5,7},{8,10},{10,12},{12,14},{9,11},... | collective-permute-start | bytes 147464 | tf_op jit(solution)/shard_map/ppermute | solution.py:23
  57.1 6.0 %collective-permute-start.2 = (bf16[6,1,32,128]{3,2,1,0:T(8,128)(2,1)S(1)}, bf16[6,1,32,128]{3,2,1,0:T(8,128)(2,1)S(1)}, u32[]{:S(2)}, u32[]{:S(2)}) collective-permute-start(bf16[6,1,32,128]{3,2,1,0:T(8,128)(2,1)S(1)} %get-tuple-element.38), channel_id=1, source_target_pairs={{2,0},{4,2},{6,4},{3,1},{5,3},{7,5},{10,8},{12,10},{14,12},{11,9},... | collective-permute-start | bytes 147464 | tf_op jit(solution)/shard_map/ppermute | solution.py:25
  63.2 2.6 %collective-permute-start.3 = (bf16[6,18,1,128]{3,2,1,0:T(2,128)(2,1)S(1)}, bf16[6,18,1,128]{3,2,1,0:T(2,128)(2,1)S(1)}, u32[]{:S(2)}, u32[]{:S(2)}) collective-permute-start(bf16[6,18,1,128]{3,2,1,0:T(2,128)(2,1)S(1)} %get-tuple-element.33), channel_id=1, source_target_pairs={{0,1},{2,3},{4,5},{6,7},{8,9},{10,11},{12,13},{14,15},{16,17},{18,... | collective-permute-start | bytes 82952 | tf_op jit(solution)/shard_map/ppermute | solution.py:23
  64.5 3.1 %collective-permute-start.4 = (bf16[6,18,1,128]{3,2,1,0:T(2,128)(2,1)S(1)}, bf16[6,18,1,128]{3,2,1,0:T(2,128)(2,1)S(1)}, u32[]{:S(2)}, u32[]{:S(2)}) collective-permute-start(bf16[6,18,1,128]{3,2,1,0:T(2,128)(2,1)S(1)} %get-tuple-element.34), channel_id=1, source_target_pairs={{1,0},{3,2},{5,4},{7,6},{9,8},{11,10},{13,12},{15,14},{17,16},{19,... | collective-permute-start | bytes 82952 | tf_op jit(solution)/shard_map/ppermute | solution.py:25
  72.1 2.2 %copy-start.1 = (bf16[3,3,3,128,128]{4,3,2,1,0:T(8,128)(2,1)S(1)}, bf16[3,3,3,128,128]{4,3,2,1,0:T(8,128)(2,1)}, u32[]{:S(2)}) copy-start(bf16[3,3,3,128,128]{4,3,2,1,0:T(8,128)(2,1)} %param.10) | copy-start | bytes 2654212
  78.9 42.4 %copy-start.3 = (f32[128]{0:T(128)S(1)}, f32[128]{0:T(128)}, u32[]{:S(2)}) copy-start(f32[128]{0:T(128)} %param.12) | copy-start | bytes 1540
  79.0 42.4 %copy-start.4 = (f32[128]{0:T(128)S(1)}, f32[128]{0:T(128)}, u32[]{:S(2)}) copy-start(f32[128]{0:T(128)} %param.11) | copy-start | bytes 1540
  121.7 7.0 %collective-permute-start.5 = (bf16[2,16,32,128]{3,2,1,0:T(8,128)(2,1)S(1)}, bf16[2,16,32,128]{3,2,1,0:T(8,128)(2,1)S(1)}, u32[]{:S(2)}, u32[]{:S(2)}) collective-permute-start(bf16[2,16,32,128]{3,2,1,0:T(8,128)(2,1)S(1)} %slice.223), channel_id=1, source_target_pairs={{0,8},{8,16},{16,24},{1,9},{9,17},{17,25},{2,10},{10,18},{18,26},{... | collective-permute-start | bytes 786440 | tf_op jit(solution)/shard_map/ppermute | solution.py:12
  128.8 6.3 %collective-permute-start.6 = (bf16[6,1,32,128]{3,2,1,0:T(8,128)(2,1)S(1)}, bf16[6,1,32,128]{3,2,1,0:T(8,128)(2,1)S(1)}, u32[]{:S(2)}, u32[]{:S(2)}) collective-permute-start(bf16[6,1,32,128]{3,2,1,0:T(8,128)(2,1)S(1)} %get-tuple-element.35), channel_id=1, source_target_pairs={{0,2},{2,4},{4,6},{1,3},{3,5},{5,7},{8,10},{10,12},{12,14},{9,11},... | collective-permute-start | bytes 147464 | tf_op jit(solution)/shard_map/ppermute | solution.py:23
  133.4 6.0 %collective-permute-start.7 = (bf16[6,1,32,128]{3,2,1,0:T(8,128)(2,1)S(1)}, bf16[6,1,32,128]{3,2,1,0:T(8,128)(2,1)S(1)}, u32[]{:S(2)}, u32[]{:S(2)}) collective-permute-start(bf16[6,1,32,128]{3,2,1,0:T(8,128)(2,1)S(1)} %get-tuple-element.36), channel_id=1, source_target_pairs={{2,0},{4,2},{6,4},{3,1},{5,3},{7,5},{10,8},{12,10},{14,12},{11,9},... | collective-permute-start | bytes 147464 | tf_op jit(solution)/shard_map/ppermute | solution.py:25
  139.5 2.8 %collective-permute-start.8 = (bf16[6,18,1,128]{3,2,1,0:T(2,128)(2,1)S(1)}, bf16[6,18,1,128]{3,2,1,0:T(2,128)(2,1)S(1)}, u32[]{:S(2)}, u32[]{:S(2)}) collective-permute-start(bf16[6,18,1,128]{3,2,1,0:T(2,128)(2,1)S(1)} %get-tuple-element.31), channel_id=1, source_target_pairs={{0,1},{2,3},{4,5},{6,7},{8,9},{10,11},{12,13},{14,15},{16,17},{18,... | collective-permute-start | bytes 82952 | tf_op jit(solution)/shard_map/ppermute | solution.py:23
  140.8 3.1 %collective-permute-start.9 = (bf16[6,18,1,128]{3,2,1,0:T(2,128)(2,1)S(1)}, bf16[6,18,1,128]{3,2,1,0:T(2,128)(2,1)S(1)}, u32[]{:S(2)}, u32[]{:S(2)}) collective-permute-start(bf16[6,18,1,128]{3,2,1,0:T(2,128)(2,1)S(1)} %get-tuple-element.32), channel_id=1, source_target_pairs={{1,0},{3,2},{5,4},{7,6},{9,8},{11,10},{13,12},{15,14},{17,16},{19,... | collective-permute-start | bytes 82952 | tf_op jit(solution)/shard_map/ppermute | solution.py:25
  148.4 2.2 %copy-start.2 = (bf16[3,3,3,128,128]{4,3,2,1,0:T(8,128)(2,1)S(1)}, bf16[3,3,3,128,128]{4,3,2,1,0:T(8,128)(2,1)}, u32[]{:S(2)}) copy-start(bf16[3,3,3,128,128]{4,3,2,1,0:T(8,128)(2,1)} %param.13) | copy-start | bytes 2654212
  155.2 1.0 copy-start
where the time goes:
time: 158 us; the launch traced here: 157 us
  blocking collectives  82.7 us (52%)
  waiting for transfers between devices  22.3 us (14%)
  starting transfers between devices  21.6 us (14%)
  other arithmetic  13.7 us (9%)
  matrix products  10.8 us (7%)
  local copies, waits for them, and re-layouts  5.8 us (4%)
    psum x2, blocking collectives, group_moments(): lax.psum((group_totals(interior), group_totals(interior * interior)), ('s...  82.7 us
    ppermute x4, waiting for transfers between devices, extended(): lax.ppermute(head, axis, [((i + 1) % count, i) for i in range(ends)])  12 us
    dot_general x18, matrix products, causal_conv(): jnp.dot(window, taps[dt, dh], preferred_element_type=jnp.float32)  10.8 us
    ppermute x4, starting transfers between devices, extended(): lax.ppermute(tail, axis, [(i, (i + 1) % count) for i in range(ends)])  10.5 us
    ppermute x2, waiting for transfers between devices, passed_along(): lax.ppermute(value, axis, [(source, source + steps) for source in range(i...  9.44 us
    concatenate x2, other arithmetic, causal_conv(): jnp.concatenate([padded[:, :, d:d + cols, :] for d in range(3)], axis=-1)  8.93 us
    ppermute x2, starting transfers between devices, passed_along(): lax.ppermute(value, axis, [(source, source + steps) for source in range(i...  5.73 us
    ppermute x4, starting transfers between devices, extended(): lax.ppermute(head, axis, [((i + 1) % count, i) for i in range(ends)])  5.35 us
  transfers between devices with their start and end apart: 10, of which 8 were waited for; matrix products, arithmetic and copies ran while one was open for 0% of the time, Pallas kernels for 0%

commit v1 on v0

v1 whole, which is shorter than its diff:
```python
import functools

import jax
import jax.numpy as jnp
from jax import lax
from jax.experimental import pallas as pl
from jax.experimental.pallas import tpu as pltpu
from jax.sharding import PartitionSpec as P

GROUPS = 32
LEAD = 8
AXES = ("section", "th", "tw")
SENDS = [(s, h, w) for s in (1, 0) for h in (0, -1, 1) for w in (0, -1, 1) if (s, h, w) != (0, 0, 0)]


def group_sum(row, per_group):
    lane = lax.broadcasted_iota(jnp.int32, row.shape, 1)
    chans = row.shape[1]
    step = 1
    while step < per_group:
        upper = lax.rem(lax.div(lane, step), 2) == 1
        row = row + jnp.where(upper, pltpu.roll(row, step, 1), pltpu.roll(row, chans - step, 1))
        step *= 2
    return row


def body(
    sizes, feat_hbm, gain1, shift1, k1_hbm, gain2, shift2, k2_hbm, out_hbm,
    feat, raw, result, hid, padded, cells, w1, w2, cols, frames_in, rows_in, cols_in, corners_in,
    mine, theirs, load_sem, out_sem, stat_send, stat_recv, halo_send, halo_recv,
):
    ns, nh, nw = sizes
    ndev = ns * nh * nw
    T, H, W, C = feat.shape
    PW = padded.shape[2]
    area = H * W
    flat = padded.reshape(padded.shape[0] * padded.shape[1] * PW, C)
    sec, th, tw = (lax.axis_index(a) for a in AXES)
    rank = (sec * nh + th) * nw + tw
    taps = k1_hbm.shape[0]
    third = taps // 3

    load = pltpu.make_async_copy(feat_hbm, feat, load_sem.at[0])
    load.start()
    weight_loads = []
    for n, (src, dst) in enumerate(((k1_hbm, w1), (k2_hbm, w2))):
        for half in range(2):
            weight_loads.append(
                pltpu.make_async_copy(
                    src,
                    dst.at[pl.ds(half * third, taps), pl.ds(half * C, C)],
                    load_sem.at[1 + 2 * n + half],
                )
            )

    def peer(d):
        other = lax.rem(rank + d, ndev)
        return (lax.div(other, nh * nw), lax.rem(lax.div(other, nw), nh), lax.rem(other, nw))

    barrier = pltpu.get_barrier_semaphore()

    def greet(d, c):
        pl.semaphore_signal(barrier, inc=1, device_id=peer(d), device_id_type=pl.DeviceIdType.MESH)
        return c

    lax.fori_loop(1, ndev, greet, 0)
    for w in weight_loads:
        w.start()
    for w in (w1, w2):
        w[3 * third : 4 * third, 0:C] = jnp.zeros((third, C), jnp.bfloat16)
        w[0:third, C : 2 * C] = jnp.zeros((third, C), jnp.bfloat16)

    def present(s, h, w):
        ok = True
        for v, at, count in ((s, sec, ns), (h, th, nh), (w, tw, nw)):
            if v < 0:
                ok = jnp.logical_and(ok, at > 0)
            if v > 0:
                ok = jnp.logical_and(ok, at < count - 1)
        return ok

    def halo_copy(n, k):
        s, h, w = SENDS[k]
        frames = pl.ds(T - 2, 2) if s else pl.ds(0, T)
        into = pl.ds(0, 2) if s else pl.ds(2, T)
        source = feat if n == 0 else raw
        hs, ws = (0 if h > 0 else 1), (0 if w > 0 else 1)
        if h == 0 and w == 0:
            src, dst = source.at[frames], frames_in.at[n]
        elif w == 0:
            src = source.at[frames, H - 1 if h > 0 else 0]
            dst = rows_in.at[n, hs, into]
        else:
            src = cols.at[n, 1 if w > 0 else 0, frames]
            dst = cols_in.at[n, ws, into] if h == 0 else corners_in.at[n, hs, ws, into]
        return pltpu.make_async_remote_copy(
            src_ref=src, dst_ref=dst,
            send_sem=halo_send.at[n, k], recv_sem=halo_recv.at[n, k],
            device_id=(sec + s, th + h, tw + w), device_id_type=pl.DeviceIdType.MESH,
        )

    def send_halo(n, which):
        for k, (s, h, w) in enumerate(SENDS):
            if s == which:
                @pl.when(present(s, h, w))
                def _():
                    halo_copy(n, k).start()

    def wait_halo(n, recv):
        for k, (s, h, w) in enumerate(SENDS):
            @pl.when(present(-s, -h, -w) if recv else present(s, h, w))
            def _():
                if recv:
                    halo_copy(n, k).wait_recv()
                else:
                    halo_copy(n, k).wait_send()

    def stat_copy(n, d):
        return pltpu.make_async_remote_copy(
            src_ref=mine.at[n], dst_ref=theirs.at[n, d - 1],
            send_sem=stat_send.at[n], recv_sem=stat_recv.at[n],
            device_id=peer(d), device_id_type=pl.DeviceIdType.MESH,
        )

    lane = lax.broadcasted_iota(jnp.int32, (1, C), 1)
    even = lax.rem(lane, 2) == 0

    def send_stats(n, total, squares):
        total = group_sum(jnp.sum(total, axis=0, keepdims=True), C // GROUPS)
        squares = group_sum(jnp.sum(squares, axis=0, keepdims=True), C // GROUPS)
        mine[n] = jnp.where(even, total, squares)

        def start(d, c):
            stat_copy(n, d).start()
            return c

        lax.fori_loop(1, ndev, start, 0)

    def all_stats(n, of):
        return pltpu.make_async_copy(theirs.at[n], theirs.at[n], of.at[n])

    def get_affine(n, gain, shift):
        all_stats(n, stat_recv).wait()
        both = jnp.sum(theirs[n], axis=0) + mine[n]
        total = jnp.where(even, both, pltpu.roll(both, 1, 1))
        squares = jnp.where(even, pltpu.roll(both, C - 1, 1), both)
        count = T * area * (C // GROUPS) * ndev
        mean = total / count
        var = squares / count - mean * mean
        scale = gain[...] / jnp.sqrt(var + 1e-06)
        return 0.5 * scale, 0.5 * (shift[...] - mean * scale)

    def fold(v):
        return jnp.sum(v.reshape(-1, 8, C), axis=0)

    load.wait()

    def first(t, carry):
        v = feat[t].astype(jnp.float32).reshape(area, C)
        hid[pl.ds(t * area, area), :] = v
        return carry[0] + fold(v), carry[1] + fold(v * v)

    zero = jnp.zeros((8, C), jnp.float32)
    sums = lax.fori_loop(0, T, first, (zero, zero))

    def take_cols(n):
        for side, j in ((0, 0), (1, W - 1)):
            edge = hid[pl.ds(j, T * H, stride=W), :]
            cols[n, side] = edge.astype(jnp.bfloat16).reshape(T, H, C)

    take_cols(0)
    pl.semaphore_wait(barrier, ndev - 1)
    send_stats(0, *sums)
    send_halo(0, 1)
    send_halo(0, 0)

    def activate(n, gain, shift):
        wait_halo(n, True)
        scale, bias = get_affine(n, gain, shift)

        def act(v):
            h = v * scale + bias
            return h * jnp.tanh(h) + h

        def inner(t, c):
            a = act(hid[pl.ds(t * area, area), :])
            padded[t + 2, 1 : H + 1, LEAD : LEAD + W] = a.reshape(H, W, C)
            return c

        lax.fori_loop(0, T, inner, 0)

        def before(t, c):
            a = act(frames_in[n, t].astype(jnp.float32).reshape(area, C))
            a = jnp.where(sec > 0, a, 0.0)
            padded[t, 1 : H + 1, LEAD : LEAD + W] = a.reshape(H, W, C)
            return c

        lax.fori_loop(0, 2, before, 0)

        def edges(t, c):
            known = jnp.logical_or(sec > 0, t >= 2)
            for hs, h in ((0, -1), (1, 1)):
                okh = jnp.logical_and(known, present(0, h, 0))
                i = 0 if hs == 0 else H + 1
                a = act(rows_in[n, hs, t].astype(jnp.float32))
                padded[t, i, LEAD : LEAD + W] = jnp.where(okh, a, 0.0)
                for ws, w in ((0, -1), (1, 1)):
                    okc = jnp.logical_and(okh, present(0, 0, w))
                    j = LEAD - 1 if ws == 0 else LEAD + W
                    a = act(corners_in[n, hs, ws, t].astype(jnp.float32))
                    a = a[H - 1 : H] if hs == 0 else a[0:1]
                    padded[t, i, j : j + 1] = jnp.where(okc, a, 0.0)
            for ws, w in ((0, -1), (1, 1)):
                okw = jnp.logical_and(known, present(0, 0, w))
                j = LEAD - 1 if ws == 0 else LEAD + W
                a = jnp.where(okw, act(cols_in[n, ws, t].astype(jnp.float32)), 0.0)
                flat[pl.ds((t * (H + 2) + 1) * PW + j, H, stride=PW), :] = a
            return c

        lax.fori_loop(0, T + 2, edges, 0)

        def shifted(t, c):
            for d in range(3):
                v = padded[t, :, LEAD - 1 + d : LEAD - 1 + d + W]
                cells[t, :, :, d * C : (d + 1) * C] = v.astype(jnp.bfloat16)
            return c

        lax.fori_loop(0, T + 2, shifted, 0)

    def conv(pair, w):
        parts = [
            cells[2 * pair + q, di : di + H].reshape(area, 3 * C)
            for q in range(4)
            for di in range(3)
        ]
        return jnp.dot(jnp.concatenate(parts, axis=-1), w[...], preferred_element_type=jnp.float32)

    activate(0, gain1, shift1)
    weight_loads[0].wait()
    weight_loads[1].wait()
    total = squares = zero
    for pair in reversed(range(T // 2)):
        both = conv(pair, w1)
        for f in range(2):
            v = both[:, f * C : (f + 1) * C]
            t = 2 * pair + f
            hid[t * area : (t + 1) * area, :] = v
            raw[t] = v.astype(jnp.bfloat16).reshape(H, W, C)
            total = total + fold(v)
            squares = squares + fold(v * v)
    take_cols(1)
    send_stats(1, total, squares)
    send_halo(1, 1)
    send_halo(1, 0)
    activate(1, gain2, shift2)
    weight_loads[2].wait()
    weight_loads[3].wait()
    stores = []
    for pair in range(T // 2):
        both = conv(pair, w2)
        for f in range(2):
            t = 2 * pair + f
            v = both[:, f * C : (f + 1) * C].reshape(H, W, C)
            result[t] = (feat[t].astype(jnp.float32) + v).astype(jnp.bfloat16)
        store = pltpu.make_async_copy(
            result.at[pl.ds(2 * pair, 2)], out_hbm.at[pl.ds(2 * pair, 2)], out_sem.at[pair]
        )
        store.start()
        stores.append(store)
    for n in range(2):
        wait_halo(n, False)
        all_stats(n, stat_send).wait()
    for store in stores:
        store.wait()


def shards(sizes, features, gain1, shift1, k1, gain2, shift2, k2):
    T, H, W, C = features.shape
    ndev = sizes[0] * sizes[1] * sizes[2]
    bf, f32 = jnp.bfloat16, jnp.float32
    any_spec = pl.BlockSpec(memory_space=pl.ANY)
    vmem = pl.BlockSpec(memory_space=pltpu.VMEM)
    flat = lambda k: k.reshape(-1, k.shape[-1])
    row = lambda v: v.reshape(1, C)
    return pl.pallas_call(
        functools.partial(body, sizes),
        out_shape=jax.ShapeDtypeStruct(features.shape, bf),
        in_specs=[any_spec, vmem, vmem, any_spec, vmem, vmem, any_spec],
        out_specs=any_spec,
        scratch_shapes=[
            pltpu.VMEM((T, H, W, C), bf),
            pltpu.VMEM((T, H, W, C), bf),
            pltpu.VMEM((T, H, W, C), bf),
            pltpu.VMEM((T * H * W, C), f32),
            pltpu.VMEM((T + 2, H + 2, W + 2 * LEAD, C), f32),
            pltpu.VMEM((T + 2, H + 2, W, 3 * C), bf),
            pltpu.VMEM((4 * 9 * C, 2 * C), bf),
            pltpu.VMEM((4 * 9 * C, 2 * C), bf),
            pltpu.VMEM((2, 2, T, H, C), bf),
            pltpu.VMEM((2, 2, H, W, C), bf),
            pltpu.VMEM((2, 2, T + 2, W, C), bf),
            pltpu.VMEM((2, 2, T + 2, H, C), bf),
            pltpu.VMEM((2, 2, 2, T + 2, H, C), bf),
            pltpu.VMEM((2, 1, C), f32),
            pltpu.VMEM((2, ndev - 1, 1, C), f32),
            pltpu.SemaphoreType.DMA((5,)),
            pltpu.SemaphoreType.DMA((T // 2,)),
            pltpu.SemaphoreType.DMA((2,)),
            pltpu.SemaphoreType.DMA((2,)),
            pltpu.SemaphoreType.DMA((2, len(SENDS))),
            pltpu.SemaphoreType.DMA((2, len(SENDS))),
        ],
        compiler_params=pltpu.CompilerParams(
            collective_id=0, has_side_effects=True, vmem_limit_bytes=60 << 20
        ),
    )(features, row(gain1), row(shift1), flat(k1), row(gain2), row(shift2), flat(k2))


def solution(mesh):
    sizes = tuple(mesh.shape[a] for a in AXES)
    placed = (P("section", "th", "tw", None), P(), P(), P(), P(), P(), P())
    return jax.shard_map(
        functools.partial(shards, sizes),
        mesh=mesh,
        in_specs=placed,
        out_specs=P("section", "th", "tw", None),
        check_vma=False,
    )
```

time: 158 us -> 35.5 us (0.22)
  the two profiles are of different devices: /device:TPU:0 before, /device:TPU:19 now
where the time goes in v1:
time: 35.5 us; the launch traced here: 35.4 us
  Pallas kernels  33.5 us (94%)
  local copies, waits for them, and re-layouts  1.87 us (5%)
    pallas_call x1, Pallas kernels, shards(): pl.pallas_call(functools.partial(body, sizes), out_shape=jax.ShapeDtypeSt...  33.5 us
    unnamed x1, local copies, waits for them, and re-layouts  1.87 us

profile of v1, /device:TPU:19, one launch (start us, length us, event | category | flops | bytes accessed | tf_op | source)
XLA Modules:
  0.0 35.4 jit_solution(11779692553738477726)
XLA Ops:
  0.0 33.5 %shard_map.73 = bf16[4,16,32,128]{3,2,1,0:T(8,128)(2,1)} custom-call(bf16[4,16,32,128]{3,2,1,0:T(8,128)(2,1)} %feat_hbm.1, f32[1,128]{1,0:T(1,128)} %bitcast.8, f32[1,128]{1,0:T(1,128)} %bitcast.9, bf16[3456,128]{1,0:T(8,128)(2,1)} %bitcast.6, f32[1,128]{1,0:T(1,128)} %bitcast.10, f32[1,128]{1,0:T(1,128)} %bitcast.11, bf16[3456,128]{1,0:T(8,128)(2,1)} %bitcast.7), custom_call_target="tpu_custom_call" | custom-call | tf_op jit(solution)/shard_map/pallas_call | solution.py:285
  33.5 1.9 %copy.9 = bf16[4,16,32,128]{3,2,1,0:T(8,128)(2,1)} copy(bf16[4,16,32,128]{3,2,1,0:T(8,128)(2,1)} %shard_map.73) | data formatting | bytes 1048576

commit v2 on v1

--- a/solution.py
+++ b/solution.py
@@ -10,7 +10,10 @@
 GROUPS = 32
 LEAD = 8
 AXES = ("section", "th", "tw")
-SENDS = [(s, h, w) for s in (1, 0) for h in (0, -1, 1) for w in (0, -1, 1) if (s, h, w) != (0, 0, 0)]
+NEAR = [(0, h, w, 0) for h in (0, -1, 1) for w in (0, -1, 1) if (h, w) != (0, 0)]
+EARLY = [(1, 0, 0, 0)]
+LATE = [(1, 0, 0, 1)] + [(1, h, w, 0) for h in (0, -1, 1) for w in (0, -1, 1) if (h, w) != (0, 0)]
+SENDS = NEAR + EARLY + LATE
 
 
 def group_sum(row, per_group):
@@ -26,7 +29,7 @@
 
 def body(
     sizes, feat_hbm, gain1, shift1, k1_hbm, gain2, shift2, k2_hbm, out_hbm,
-    feat, raw, result, hid, padded, cells, w1, w2, cols, frames_in, rows_in, cols_in, corners_in,
+    feat, raw, result, hid, padded, cells, acc, w1, w2, cols, corners, frames_in, rows_in, cols_in, corners_in,
     mine, theirs, load_sem, out_sem, stat_send, stat_recv, halo_send, halo_recv,
 ):
     ns, nh, nw = sizes
@@ -79,41 +82,53 @@
                 ok = jnp.logical_and(ok, at < count - 1)
         return ok
 
-    def halo_copy(n, k):
-        s, h, w = SENDS[k]
+    chunk = H // 2
+
+    def halo_copy(n, kind):
+        s, h, w, part = kind
+        k = SENDS.index(kind)
         frames = pl.ds(T - 2, 2) if s else pl.ds(0, T)
         into = pl.ds(0, 2) if s else pl.ds(2, T)
         source = feat if n == 0 else raw
         hs, ws = (0 if h > 0 else 1), (0 if w > 0 else 1)
         if h == 0 and w == 0:
-            src, dst = source.at[frames], frames_in.at[n]
+            if part == 0:
+                src, dst = source.at[T - 2, pl.ds(0, chunk)], frames_in.at[n, 0, pl.ds(0, chunk)]
+            else:
+                rest = pl.ds(chunk, 2 * H - chunk)
+                src = source.at[pl.ds(T - 2, 2)].reshape(2 * H, W, C).at[rest]
+                dst = frames_in.at[n].reshape(2 * H, W, C).at[rest]
         elif w == 0:
             src = source.at[frames, H - 1 if h > 0 else 0]
             dst = rows_in.at[n, hs, into]
+        elif h == 0:
+            src = cols.at[n, 1 if w > 0 else 0, frames]
+            dst = cols_in.at[n, ws, into]
         else:
-            src = cols.at[n, 1 if w > 0 else 0, frames]
-            dst = cols_in.at[n, ws, into] if h == 0 else corners_in.at[n, hs, ws, into]
+            src = corners.at[n, 1 if h > 0 else 0, 1 if w > 0 else 0, frames]
+            dst = corners_in.at[n, hs, ws, into]
         return pltpu.make_async_remote_copy(
             src_ref=src, dst_ref=dst,
             send_sem=halo_send.at[n, k], recv_sem=halo_recv.at[n, k],
             device_id=(sec + s, th + h, tw + w), device_id_type=pl.DeviceIdType.MESH,
         )
 
-    def send_halo(n, which):
-        for k, (s, h, w) in enumerate(SENDS):
-            if s == which:
-                @pl.when(present(s, h, w))
-                def _():
-                    halo_copy(n, k).start()
-
-    def wait_halo(n, recv):
-        for k, (s, h, w) in enumerate(SENDS):
+    def send_halo(n, kinds):
+        for kind in kinds:
+            @pl.when(present(*kind[:3]))
+            def _():
+                halo_copy(n, kind).start()
+
+    def wait_halo(n, kinds, recv):
+        for kind in kinds:
+            s, h, w, _part = kind
+
             @pl.when(present(-s, -h, -w) if recv else present(s, h, w))
             def _():
                 if recv:
-                    halo_copy(n, k).wait_recv()
+                    halo_copy(n, kind).wait_recv()
                 else:
-                    halo_copy(n, k).wait_send()
+                    halo_copy(n, kind).wait_send()
 
     def stat_copy(n, d):
         return pltpu.make_async_remote_copy(
@@ -163,40 +178,24 @@
     zero = jnp.zeros((8, C), jnp.float32)
     sums = lax.fori_loop(0, T, first, (zero, zero))
 
-    def take_cols(n):
+    def take_edges(n, start, count):
         for side, j in ((0, 0), (1, W - 1)):
-            edge = hid[pl.ds(j, T * H, stride=W), :]
-            cols[n, side] = edge.astype(jnp.bfloat16).reshape(T, H, C)
-
-    take_cols(0)
+            edge = hid[pl.ds(start * area + j, count * H, stride=W), :]
+            cols[n, side, start : start + count] = edge.astype(jnp.bfloat16).reshape(count, H, C)
+            for t in range(start, start + count):
+                for hside, i in ((0, 0), (1, H - 1)):
+                    at = t * area + i * W + j
+                    pixel = jnp.broadcast_to(hid[at : at + 1, :], (2, C))
+                    corners[n, hside, side, t] = pixel.astype(jnp.bfloat16)
+
+    take_edges(0, 0, T)
     pl.semaphore_wait(barrier, ndev - 1)
     send_stats(0, *sums)
-    send_halo(0, 1)
-    send_halo(0, 0)
-
-    def activate(n, gain, shift):
-        wait_halo(n, True)
-        scale, bias = get_affine(n, gain, shift)
-
-        def act(v):
-            h = v * scale + bias
-            return h * jnp.tanh(h) + h
-
-        def inner(t, c):
-            a = act(hid[pl.ds(t * area, area), :])
-            padded[t + 2, 1 : H + 1, LEAD : LEAD + W] = a.reshape(H, W, C)
-            return c
-
-        lax.fori_loop(0, T, inner, 0)
-
-        def before(t, c):
-            a = act(frames_in[n, t].astype(jnp.float32).reshape(area, C))
-            a = jnp.where(sec > 0, a, 0.0)
-            padded[t, 1 : H + 1, LEAD : LEAD + W] = a.reshape(H, W, C)
-            return c
-
-        lax.fori_loop(0, 2, before, 0)
-
+    send_halo(0, NEAR)
+    send_halo(0, EARLY)
+    send_halo(0, LATE)
+
+    def fill_edges(n, act, lo, hi):
         def edges(t, c):
             known = jnp.logical_or(sec > 0, t >= 2)
             for hs, h in ((0, -1), (1, 1)):
@@ -208,39 +207,76 @@
                     okc = jnp.logical_and(okh, present(0, 0, w))
                     j = LEAD - 1 if ws == 0 else LEAD + W
                     a = act(corners_in[n, hs, ws, t].astype(jnp.float32))
-                    a = a[H - 1 : H] if hs == 0 else a[0:1]
-                    padded[t, i, j : j + 1] = jnp.where(okc, a, 0.0)
+                    padded[t, i, j : j + 1] = jnp.where(okc, a[0:1], 0.0)
             for ws, w in ((0, -1), (1, 1)):
                 okw = jnp.logical_and(known, present(0, 0, w))
                 j = LEAD - 1 if ws == 0 else LEAD + W
                 a = jnp.where(okw, act(cols_in[n, ws, t].astype(jnp.float32)), 0.0)
                 flat[pl.ds((t * (H + 2) + 1) * PW + j, H, stride=PW), :] = a
-            return c
-
-        lax.fori_loop(0, T + 2, edges, 0)
-
-        def shifted(t, c):
             for d in range(3):
                 v = padded[t, :, LEAD - 1 + d : LEAD - 1 + d + W]
                 cells[t, :, :, d * C : (d + 1) * C] = v.astype(jnp.bfloat16)
             return c
 
-        lax.fori_loop(0, T + 2, shifted, 0)
-
-    def conv(pair, w):
-        parts = [
-            cells[2 * pair + q, di : di + H].reshape(area, 3 * C)
-            for q in range(4)
-            for di in range(3)
+        lax.fori_loop(lo, hi, edges, 0)
+
+    def own_frames(n, gain, shift):
+        scale, bias = get_affine(n, gain, shift)
+
+        def act(v):
+            h = v * scale + bias
+            return h * jnp.tanh(h) + h
+
+        def inner(t, c):
+            a = act(hid[pl.ds(t * area, area), :])
+            padded[t + 2, 1 : H + 1, LEAD : LEAD + W] = a.reshape(H, W, C)
+            return c
+
+        lax.fori_loop(0, T, inner, 0)
+        wait_halo(n, NEAR, True)
+        fill_edges(n, act, 2, T + 2)
+        return act
+
+    def halo_frames(n, act):
+        wait_halo(n, EARLY + LATE, True)
+
+        def before(t, c):
+            a = act(frames_in[n, t].astype(jnp.float32).reshape(area, C))
+            a = jnp.where(sec > 0, a, 0.0)
+            padded[t, 1 : H + 1, LEAD : LEAD + W] = a.reshape(H, W, C)
+            return c
+
+        lax.fori_loop(0, 2, before, 0)
+        fill_edges(n, act, 0, 2)
+
+    pairs = T // 2
+    half = 18 * C
+
+    def window(pair, q):
+        return [cells[2 * pair + q, di : di + H].reshape(area, 3 * C) for di in range(3)]
+
+    def conv_later(w):
+        rows = [
+            jnp.concatenate(window(pair, 2) + window(pair, 3), axis=-1) for pair in range(pairs)
         ]
-        return jnp.dot(jnp.concatenate(parts, axis=-1), w[...], preferred_element_type=jnp.float32)
-
-    activate(0, gain1, shift1)
+        acc[...] = jnp.dot(
+            jnp.concatenate(rows, axis=0), w[half : 2 * half], preferred_element_type=jnp.float32
+        )
+
+    def conv_pair(pair, w):
+        lhs = jnp.concatenate(window(pair, 0) + window(pair, 1), axis=-1)
+        part = jnp.dot(lhs, w[0:half], preferred_element_type=jnp.float32)
+        return acc[pair * area : (pair + 1) * area, :] + part
+
+    act = own_frames(0, gain1, shift1)
     weight_loads[0].wait()
     weight_loads[1].wait()
     total = squares = zero
-    for pair in reversed(range(T // 2)):
-        both = conv(pair, w1)
+    conv_later(w1)
+    for pair in reversed(range(pairs)):
+        if pair == 0:
+            halo_frames(0, act)
+        both = conv_pair(pair, w1)
         for f in range(2):
             v = both[:, f * C : (f + 1) * C]
             t = 2 * pair + f
@@ -248,16 +284,21 @@
             raw[t] = v.astype(jnp.bfloat16).reshape(H, W, C)
             total = total + fold(v)
             squares = squares + fold(v * v)
-    take_cols(1)
+        take_edges(1, 2 * pair, 2)
+        if pair == pairs - 1:
+            send_halo(1, EARLY)
     send_stats(1, total, squares)
-    send_halo(1, 1)
-    send_halo(1, 0)
-    activate(1, gain2, shift2)
+    send_halo(1, NEAR)
+    send_halo(1, LATE)
+    act = own_frames(1, gain2, shift2)
     weight_loads[2].wait()
     weight_loads[3].wait()
+    conv_later(w2)
     stores = []
-    for pair in range(T // 2):
-        both = conv(pair, w2)
+    for pair in reversed(range(pairs)):
+        if pair == 0:
+            halo_frames(1, act)
+        both = conv_pair(pair, w2)
         for f in range(2):
             t = 2 * pair + f
             v = both[:, f * C : (f + 1) * C].reshape(H, W, C)
@@ -268,7 +309,7 @@
         store.start()
         stores.append(store)
     for n in range(2):
-        wait_halo(n, False)
+        wait_halo(n, SENDS, False)
         all_stats(n, stat_send).wait()
     for store in stores:
         store.wait()
@@ -294,13 +335,15 @@
             pltpu.VMEM((T * H * W, C), f32),
             pltpu.VMEM((T + 2, H + 2, W + 2 * LEAD, C), f32),
             pltpu.VMEM((T + 2, H + 2, W, 3 * C), bf),
+            pltpu.VMEM((T // 2 * H * W, 2 * C), f32),
             pltpu.VMEM((4 * 9 * C, 2 * C), bf),
             pltpu.VMEM((4 * 9 * C, 2 * C), bf),
             pltpu.VMEM((2, 2, T, H, C), bf),
+            pltpu.VMEM((2, 2, 2, T, 2, C), bf),
             pltpu.VMEM((2, 2, H, W, C), bf),
             pltpu.VMEM((2, 2, T + 2, W, C), bf),
             pltpu.VMEM((2, 2, T + 2, H, C), bf),
-            pltpu.VMEM((2, 2, 2, T + 2, H, C), bf),
+            pltpu.VMEM((2, 2, 2, T + 2, 2, C), bf),
             pltpu.VMEM((2, 1, C), f32),
             pltpu.VMEM((2, ndev - 1, 1, C), f32),
             pltpu.SemaphoreType.DMA((5,)),

time: 35.5 us -> 32.8 us (0.924)
  the two profiles are of different devices: /device:TPU:19 before, /device:TPU:0 now
where the time goes in v2:
time: 32.8 us; the launch traced here: 32.7 us
  Pallas kernels  30.8 us (94%)
  local copies, waits for them, and re-layouts  1.87 us (6%)
    pallas_call x1, Pallas kernels, shards(): pl.pallas_call(functools.partial(body, sizes), out_shape=jax.ShapeDtypeSt...  30.8 us
    unnamed x1, local copies, waits for them, and re-layouts  1.87 us

profile of v2, /device:TPU:0, one launch (start us, length us, event | category | flops | bytes accessed | tf_op | source)
XLA Modules:
  0.0 32.7 jit_solution(10820792525590572484)
XLA Ops:
  0.0 30.8 %shard_map.73 = bf16[4,16,32,128]{3,2,1,0:T(8,128)(2,1)} custom-call(bf16[4,16,32,128]{3,2,1,0:T(8,128)(2,1)} %feat_hbm.1, f32[1,128]{1,0:T(1,128)} %bitcast.8, f32[1,128]{1,0:T(1,128)} %bitcast.9, bf16[3456,128]{1,0:T(8,128)(2,1)} %bitcast.6, f32[1,128]{1,0:T(1,128)} %bitcast.10, f32[1,128]{1,0:T(1,128)} %bitcast.11, bf16[3456,128]{1,0:T(8,128)(2,1)} %bitcast.7), custom_call_target="tpu_custom_call" | custom-call | tf_op jit(solution)/shard_map/pallas_call | solution.py:326
  30.8 1.9 %copy.9 = bf16[4,16,32,128]{3,2,1,0:T(8,128)(2,1)} copy(bf16[4,16,32,128]{3,2,1,0:T(8,128)(2,1)} %shard_map.73) | data formatting | bytes 1048576

commit v3 on v2

--- a/solution.py
+++ b/solution.py
@@ -28,9 +28,9 @@
 
 
 def body(
-    sizes, feat_hbm, gain1, shift1, k1_hbm, gain2, shift2, k2_hbm, out_hbm,
-    feat, raw, result, hid, padded, cells, acc, w1, w2, cols, corners, frames_in, rows_in, cols_in, corners_in,
-    mine, theirs, load_sem, out_sem, stat_send, stat_recv, halo_send, halo_recv,
+    sizes, feat_hbm, gain1, shift1, k1_hbm, gain2, shift2, k2_hbm, out,
+    feat, raw, hid, padded, cells, acc, w1, w2, cols, corners, frames_in, rows_in, cols_in, corners_in,
+    mine, theirs, load_sem, stat_send, stat_recv, halo_send, halo_recv,
 ):
     ns, nh, nw = sizes
     ndev = ns * nh * nw
@@ -130,15 +130,15 @@
                 else:
                     halo_copy(n, kind).wait_send()
 
+    lane = lax.broadcasted_iota(jnp.int32, (1, C), 1)
+    even = lax.rem(lane, 2) == 0
+
     def stat_copy(n, d):
         return pltpu.make_async_remote_copy(
             src_ref=mine.at[n], dst_ref=theirs.at[n, d - 1],
             send_sem=stat_send.at[n], recv_sem=stat_recv.at[n],
             device_id=peer(d), device_id_type=pl.DeviceIdType.MESH,
         )
-
-    lane = lax.broadcasted_iota(jnp.int32, (1, C), 1)
-    even = lax.rem(lane, 2) == 0
 
     def send_stats(n, total, squares):
         total = group_sum(jnp.sum(total, axis=0, keepdims=True), C // GROUPS)
@@ -250,23 +250,26 @@
         fill_edges(n, act, 0, 2)
 
     pairs = T // 2
-    half = 18 * C
-
-    def window(pair, q):
-        return [cells[2 * pair + q, di : di + H].reshape(area, 3 * C) for di in range(3)]
+    early = 20 * C
+
+    def window(pair, q, di, lo=0, hi=3):
+        return cells[2 * pair + q, di : di + H, :, lo * C : hi * C].reshape(area, (hi - lo) * C)
+
+    def stacked(some, *where):
+        return jnp.concatenate([window(pair, *where) for pair in some], axis=0)
 
     def conv_later(w):
-        rows = [
-            jnp.concatenate(window(pair, 2) + window(pair, 3), axis=-1) for pair in range(pairs)
-        ]
-        acc[...] = jnp.dot(
-            jnp.concatenate(rows, axis=0), w[half : 2 * half], preferred_element_type=jnp.float32
-        )
-
-    def conv_pair(pair, w):
-        lhs = jnp.concatenate(window(pair, 0) + window(pair, 1), axis=-1)
-        part = jnp.dot(lhs, w[0:half], preferred_element_type=jnp.float32)
-        return acc[pair * area : (pair + 1) * area, :] + part
+        some = range(pairs)
+        parts = [stacked(some, 2, 0, 2, 3), stacked(some, 2, 1), stacked(some, 2, 2)]
+        parts += [stacked(some, 3, di) for di in range(3)]
+        lhs = jnp.concatenate(parts, axis=-1)
+        acc[...] = jnp.dot(lhs, w[early:], preferred_element_type=jnp.float32)
+
+    def conv_first(some, w):
+        parts = [stacked(some, q, di) for q in range(2) for di in range(3)]
+        lhs = jnp.concatenate(parts + [stacked(some, 2, 0, 0, 2)], axis=-1)
+        part = jnp.dot(lhs, w[0:early], preferred_element_type=jnp.float32)
+        return acc[some[0] * area : (some[-1] + 1) * area, :] + part
 
     act = own_frames(0, gain1, shift1)
     weight_loads[0].wait()
@@ -276,7 +279,7 @@
     for pair in reversed(range(pairs)):
         if pair == 0:
             halo_frames(0, act)
-        both = conv_pair(pair, w1)
+        both = conv_first([pair], w1)
         for f in range(2):
             v = both[:, f * C : (f + 1) * C]
             t = 2 * pair + f
@@ -294,25 +297,18 @@
     weight_loads[2].wait()
     weight_loads[3].wait()
     conv_later(w2)
-    stores = []
     for pair in reversed(range(pairs)):
         if pair == 0:
             halo_frames(1, act)
-        both = conv_pair(pair, w2)
+        both = conv_first([pair], w2)
         for f in range(2):
             t = 2 * pair + f
             v = both[:, f * C : (f + 1) * C].reshape(H, W, C)
-            result[t] = (feat[t].astype(jnp.float32) + v).astype(jnp.bfloat16)
-        store = pltpu.make_async_copy(
-            result.at[pl.ds(2 * pair, 2)], out_hbm.at[pl.ds(2 * pair, 2)], out_sem.at[pair]
-        )
-        store.start()
-        stores.append(store)
+            out[t] = (feat[t].astype(jnp.float32) + v).astype(jnp.bfloat16)
     for n in range(2):
         wait_halo(n, SENDS, False)
+    for n in range(2):
         all_stats(n, stat_send).wait()
-    for store in stores:
-        store.wait()
 
 
 def shards(sizes, features, gain1, shift1, k1, gain2, shift2, k2):
@@ -325,11 +321,10 @@
     row = lambda v: v.reshape(1, C)
     return pl.pallas_call(
         functools.partial(body, sizes),
-        out_shape=jax.ShapeDtypeStruct(features.shape, bf),
+        out_shape=pltpu.VMEM(features.shape, bf),
         in_specs=[any_spec, vmem, vmem, any_spec, vmem, vmem, any_spec],
-        out_specs=any_spec,
+        out_specs=vmem,
         scratch_shapes=[
-            pltpu.VMEM((T, H, W, C), bf),
             pltpu.VMEM((T, H, W, C), bf),
             pltpu.VMEM((T, H, W, C), bf),
             pltpu.VMEM((T * H * W, C), f32),
@@ -347,7 +342,6 @@
             pltpu.VMEM((2, 1, C), f32),
             pltpu.VMEM((2, ndev - 1, 1, C), f32),
             pltpu.SemaphoreType.DMA((5,)),
-            pltpu.SemaphoreType.DMA((T // 2,)),
             pltpu.SemaphoreType.DMA((2,)),
             pltpu.SemaphoreType.DMA((2,)),
             pltpu.SemaphoreType.DMA((2, len(SENDS))),

time: 32.8 us -> 31.1 us (0.948)
  local copies, waits for them, and re-layouts: 1.87 us -> 0.8 us
  Pallas kernels: 30.8 us -> 30.1 us
    unnamed x1, local copies, waits for them, and re-layouts: 1.87 us -> 0.8 us
    pallas_call x1, Pallas kernels: 30.8 us -> 30.1 us  [shards(): pl.pallas_call(functools.partial(body, sizes), out_shape=pltpu.VMEM(featu...]
where the time goes in v3:
time: 31.1 us; the launch traced here: 30.9 us
  Pallas kernels  30.1 us (97%)
  local copies, waits for them, and re-layouts  0.8 us (3%)
    pallas_call x1, Pallas kernels, shards(): pl.pallas_call(functools.partial(body, sizes), out_shape=pltpu.VMEM(featu...  30.1 us
    unnamed x1, local copies, waits for them, and re-layouts  0.8 us

profile of v3, /device:TPU:0, one launch (start us, length us, event | category | flops | bytes accessed | tf_op | source)
XLA Modules:
  0.0 30.9 jit_solution(14083658331766971110)
XLA Ops:
  0.0 30.1 %shard_map.73 = bf16[4,16,32,128]{3,2,1,0:T(8,128)(2,1)S(1)} custom-call(bf16[4,16,32,128]{3,2,1,0:T(8,128)(2,1)} %feat_hbm.1, f32[1,128]{1,0:T(1,128)} %bitcast.8, f32[1,128]{1,0:T(1,128)} %bitcast.9, bf16[3456,128]{1,0:T(8,128)(2,1)} %bitcast.6, f32[1,128]{1,0:T(1,128)} %bitcast.10, f32[1,128]{1,0:T(1,128)} %bitcast.11, bf16[3456,128]{1,0:T(8,128)(2,1)} %bitcast.7), custom_call_target="tpu_custom_call" | custom-call | tf_op jit(solution)/shard_map/pallas_call | solution.py:322
  30.1 0.8 %copy.9 = bf16[4,16,32,128]{3,2,1,0:T(8,128)(2,1)} copy(bf16[4,16,32,128]{3,2,1,0:T(8,128)(2,1)S(1)} %shard_map.73) | data formatting | bytes 1048576

commit v4 on v3

--- a/solution.py
+++ b/solution.py
@@ -263,7 +263,8 @@
         parts = [stacked(some, 2, 0, 2, 3), stacked(some, 2, 1), stacked(some, 2, 2)]
         parts += [stacked(some, 3, di) for di in range(3)]
         lhs = jnp.concatenate(parts, axis=-1)
-        acc[...] = jnp.dot(lhs, w[early:], preferred_element_type=jnp.float32)
+        for m in range(pairs):
+            acc[m * area : (m + 1) * area, :] = jnp.dot(lhs[m * area : (m + 1) * area], w[early:], preferred_element_type=jnp.float32)
 
     def conv_first(some, w):
         parts = [stacked(some, q, di) for q in range(2) for di in range(3)]

time: 31.1 us -> 29.5 us (0.949)
  Pallas kernels: 30.1 us -> 28.6 us
    pallas_call x1, Pallas kernels: 30.1 us -> 28.6 us  [shards(): pl.pallas_call(functools.partial(body, sizes), out_shape=pltpu.VMEM(featu...]
where the time goes in v4:
time: 29.5 us; the launch traced here: 29.4 us
  Pallas kernels  28.6 us (97%)
  local copies, waits for them, and re-layouts  0.8 us (3%)
    pallas_call x1, Pallas kernels, shards(): pl.pallas_call(functools.partial(body, sizes), out_shape=pltpu.VMEM(featu...  28.6 us
    unnamed x1, local copies, waits for them, and re-layouts  0.8 us

profile of v4, /device:TPU:0, one launch (start us, length us, event | category | flops | bytes accessed | tf_op | source)
XLA Modules:
  0.0 29.4 jit_solution(2409390455871907655)
XLA Ops:
  0.0 28.6 %shard_map.73 = bf16[4,16,32,128]{3,2,1,0:T(8,128)(2,1)S(1)} custom-call(bf16[4,16,32,128]{3,2,1,0:T(8,128)(2,1)} %feat_hbm.1, f32[1,128]{1,0:T(1,128)} %bitcast.8, f32[1,128]{1,0:T(1,128)} %bitcast.9, bf16[3456,128]{1,0:T(8,128)(2,1)} %bitcast.6, f32[1,128]{1,0:T(1,128)} %bitcast.10, f32[1,128]{1,0:T(1,128)} %bitcast.11, bf16[3456,128]{1,0:T(8,128)(2,1)} %bitcast.7), custom_call_target="tpu_custom_call" | custom-call | tf_op jit(solution)/shard_map/pallas_call | solution.py:323
  28.6 0.8 %copy.9 = bf16[4,16,32,128]{3,2,1,0:T(8,128)(2,1)} copy(bf16[4,16,32,128]{3,2,1,0:T(8,128)(2,1)S(1)} %shard_map.73) | data formatting | bytes 1048576
